TPU v7x, 32 devices: a whole 2x2x4 slice. The times are simulated.
32 devices in a mesh: dp: 4 (over y, core), tensor: 8 (over z, x).
Axes of the slice: x: 2, y: 2, z: 4, core: 2. Of those that a mesh axis runs over, the one named last changes fastest.
Arguments:
- tokens: bfloat16 [3072, 8192], P('dp', 'tensor'), may hold values from -6 to 6
- cotangent: bfloat16 [3072, 512], P('dp', 'tensor'), may hold values from -0.0625 to 0.0625
- frozen_value_weight: bfloat16 [8192, 512], P('tensor'), may hold values from -0.0625 to 0.0625
- adapter_down_weight: bfloat16 [8, 32, 8192], P('tensor'), may hold values from -0.0625 to 0.0625
- adapter_up_weight: bfloat16 [8, 32, 512], P('tensor'), may hold values from -1 to 1
- member: int32 [24, 1], P('dp'), may hold values from 0 to 7; in each aligned block of 6 rows (0 to 5, 6 to 11, ...) at most 2 rows name the same one
Outputs:
- output: bfloat16 [3072, 512], P(('dp', 'tensor'))
- grad_down: float32 [8, 32, 8192], P('tensor', None, 'dp')
- grad_up: float32 [8, 32, 512], P('tensor', 'dp')
Inputs may be any that keep to these rules, and one draw needn't show every extreme that they name: Within the 6 blocks of one data index no member appears more than 2 times, and some member appears exactly 2 times there.
All inputs are finite; a program needn't handle non-finite values.
Results may differ from a plain program's by a relative error of at most 0.015.
Values may be sent and summed in bfloat16 or wider, within the bound.
A program may use at most 64 MiB of HBM per device.

v0:
```python
import jax
import jax.numpy as jnp
from jax import lax
from jax.sharding import PartitionSpec as P

BLK = 128
CAP = 2
adapter_scale = 2.0
contract_trailing = (((1,), (1,)), ((), ()))
contract_leading = (((0,), (0,)), ((), ()))


def slot_table(member_ids, tensor_size):
    block_total = member_ids.shape[0]
    position = jnp.arange(block_total, dtype=jnp.int32)
    same_member = member_ids[:, None] == member_ids[None, :]
    earlier = position[None, :] < position[:, None]
    slot_rank = jnp.sum(jnp.logical_and(same_member, earlier), axis=1)
    owners = jnp.arange(tensor_size, dtype=jnp.int32)
    slot_numbers = jnp.arange(CAP, dtype=jnp.int32)
    picked = jnp.logical_and(
        member_ids[None, None, :] == owners[:, None, None],
        slot_rank[None, None, :] == slot_numbers[None, :, None],
    )
    return picked.astype(jnp.bfloat16)


def shards(tokens, cotangent, frozen_value_weight, adapter_down_weight, adapter_up_weight, member):
    tensor_size = lax.axis_size("tensor")
    owner_index = lax.axis_index("tensor")
    row_total = tokens.shape[0]
    feature_width = tokens.shape[1]
    cot_width = cotangent.shape[1]
    out_width = frozen_value_weight.shape[1]
    block_total = row_total // BLK
    own_rows = row_total // tensor_size
    member_ids = member[:, 0]
    picked = slot_table(member_ids, tensor_size)
    flat_picked = picked.reshape(tensor_size * CAP, block_total)
    token_blocks = tokens.reshape(block_total, BLK * feature_width)
    cot_blocks = cotangent.reshape(block_total, BLK * cot_width)
    send_tokens = jnp.dot(flat_picked, token_blocks, preferred_element_type=jnp.float32).astype(
        jnp.bfloat16
    )
    send_tokens = send_tokens.reshape(tensor_size, CAP * BLK, feature_width)
    send_cot = jnp.dot(flat_picked, cot_blocks, preferred_element_type=jnp.float32).astype(
        jnp.bfloat16
    )
    send_cot = send_cot.reshape(tensor_size, CAP * BLK, cot_width)
    got_tokens, got_cot = (
        lax.all_to_all(send_tokens, "tensor", split_axis=0, concat_axis=2, tiled=True),
        lax.all_to_all(send_cot, "tensor", split_axis=0, concat_axis=2, tiled=True),
    )
    slot_tokens = got_tokens[0]
    slot_cot = got_cot[0]
    down_projection = adapter_down_weight[0]
    up_projection = adapter_up_weight[0]
    hidden_state = lax.dot_general(
        slot_tokens, down_projection, contract_trailing, preferred_element_type=jnp.float32
    ).astype(jnp.bfloat16)
    adapter_result = (
        adapter_scale * jnp.dot(hidden_state, up_projection, preferred_element_type=jnp.float32)
    ).astype(jnp.bfloat16)
    backward_projection = (
        adapter_scale
        * lax.dot_general(
            slot_cot, up_projection, contract_trailing, preferred_element_type=jnp.float32
        )
    ).astype(jnp.bfloat16)
    local_down = lax.dot_general(
        backward_projection, slot_tokens, contract_leading, preferred_element_type=jnp.float32
    )
    member_up_weight = adapter_scale * lax.dot_general(
        hidden_state, slot_cot, contract_leading, preferred_element_type=jnp.float32
    )
    base_total = lax.psum_scatter(
        jnp.dot(tokens, frozen_value_weight, preferred_element_type=jnp.float32).astype(
            jnp.bfloat16
        ),
        "tensor",
        scatter_dimension=0,
        tiled=True,
    ).astype(jnp.float32)
    my_slots = lax.dynamic_index_in_dim(picked, owner_index, 0, keepdims=False)
    placed = jnp.dot(
        my_slots.T, adapter_result.reshape(CAP, BLK * out_width), preferred_element_type=jnp.float32
    ).astype(jnp.bfloat16)
    placed = placed.reshape(tensor_size, own_rows, out_width)
    returned = lax.all_to_all(placed, "tensor", split_axis=0, concat_axis=0, tiled=True)
    adapter_rows = jnp.sum(returned.astype(jnp.float32), axis=0)
    output = (base_total + adapter_rows).astype(jnp.bfloat16)
    grad_down, grad_up = (
        lax.psum_scatter(
            local_down[None].astype(jnp.bfloat16), "dp", scatter_dimension=2, tiled=True
        ).astype(jnp.float32),
        lax.psum_scatter(
            member_up_weight[None].astype(jnp.bfloat16), "dp", scatter_dimension=1, tiled=True
        ).astype(jnp.float32),
    )
    return (output, grad_down, grad_up)


def solution(mesh):
    placed = (
        P("dp", "tensor"),
        P("dp", "tensor"),
        P("tensor", None),
        P("tensor", None, None),
        P("tensor", None, None),
        P("dp", None),
    )
    return jax.shard_map(
        shards,
        mesh=mesh,
        in_specs=placed,
        out_specs=(P(("dp", "tensor"), None), P("tensor", None, "dp"), P("tensor", "dp", None)),
        check_vma=False,
    )
```

profile of v0, /device:TPU:0, one launch (start us, length us, event | category | flops | bytes accessed | tf_op | source)
XLA Modules:
  0.0 258.6 jit_solution(10288526673390440713)
XLA Ops:
  7.2 0.8 iota_compare_fusion.1
  7.9 0.9 convert_reduce_fusion.1
  8.9 3.4 %reshape.95 = bf16[6,131072]{1,0:T(8,128)(2,1)S(1)} reshape(bf16[768,1024]{1,0:T(8,128)(2,1)} %param.6) | data formatting | bytes 3145728 | tf_op jit(solution)/shard_map/reshape | solution.py:40
  12.2 3.2 %convolution_convert_fusion = bf16[16,131072]{1,0:T(8,128)(2,1)} fusion(pred[16,6]{1,0:T(8,128)(4,1)S(1)} %and.35, bf16[6,131072]{1,0:T(8,128)(2,1)S(1)} %reshape.95), kind=kOutput, calls=%fused_computation | convolution fusion | flops 27262976 | bytes 5767264 | tf_op jit(solution)/shard_map/dot_general | solution.py:42
  15.5 4.8 %reshape.96 = bf16[8,256,1024]{2,1,0:T(8,128)(2,1)} reshape(bf16[16,131072]{1,0:T(8,128)(2,1)} %convolution_convert_fusion) | data formatting | bytes 8388608 | tf_op jit(solution)/shard_map/reshape | solution.py:45
  20.3 6.5 %copy.15 = bf16[8,256,1024]{1,2,0:T(8,128)(2,1)} copy(bf16[8,256,1024]{2,1,0:T(8,128)(2,1)} %reshape.96) | data formatting | bytes 8388608 | tf_op jit(solution)/shard_map/reshape | solution.py:45
  26.8 7.4 %all-to-all-start = ((bf16[8,256,1024]{1,2,0:T(8,128)(2,1)}), bf16[8,256,1024]{1,2,0:T(8,128)(2,1)}, u32[]{:S(2)}, u32[]{:S(2)}) async-start(bf16[8,256,1024]{1,2,0:T(8,128)(2,1)} %copy.15), calls=%async_computation.1 | async-start | bytes 8388608 | tf_op jit(solution)/shard_map/all_to_all | solution.py:51
  34.8 0.5 reshape.100
  35.3 0.9 copy.17
  36.2 91.2 %all-to-all-done = bf16[8,256,1024]{1,2,0:T(8,128)(2,1)} async-done(((bf16[8,256,1024]{1,2,0:T(8,128)(2,1)}), bf16[8,256,1024]{1,2,0:T(8,128)(2,1)}, u32[]{:S(2)}, u32[]{:S(2)}) %all-to-all-start) | async-done | bytes 4194336 | tf_op jit(solution)/shard_map/all_to_all | solution.py:51
  127.5 3.6 %all-to-all-start.2 = ((bf16[8,256,64]{1,2,0:T(8,128)(2,1)}), bf16[8,256,64]{1,2,0:T(8,128)(2,1)S(1)}, u32[]{:S(2)}, u32[]{:S(2)}) async-start(bf16[8,256,64]{1,2,0:T(8,128)(2,1)} %copy.17), calls=%async_computation.3 | async-start | bytes 524288 | tf_op jit(solution)/shard_map/all_to_all | solution.py:52
  131.2 3.1 %convolution_convert_fusion.5 = bf16[256,32]{0,1:T(8,128)(2,1)S(1)} fusion(bf16[256,8192]{0,1:T(8,128)(2,1)} %bitcast.4, bf16[1,32,8192]{2,1,0:T(8,128)(2,1)S(1)} %copy-done.2), kind=kOutput, calls=%fused_computation.14 | convolution fusion | flops 134225920 | bytes 4734976 | tf_op jit(solution)/shard_map/dot_general | solution.py:58
  134.3 5.9 %all-to-all-done.2 = bf16[8,256,64]{1,2,0:T(8,128)(2,1)S(1)} async-done(((bf16[8,256,64]{1,2,0:T(8,128)(2,1)}), bf16[8,256,64]{1,2,0:T(8,128)(2,1)S(1)}, u32[]{:S(2)}, u32[]{:S(2)}) %all-to-all-start.2) | async-done | bytes 262176 | tf_op jit(solution)/shard_map/all_to_all | solution.py:52
  140.2 0.8 fusion.3
  141.1 4.4 %fusion = bf16[1,32,8192]{2,1,0:T(8,128)(2,1)} fusion(bf16[256,8192]{0,1:T(8,128)(2,1)} %bitcast.4, bf16[256,512]{0,1:T(8,128)(2,1)S(1)} %bitcast.41, bf16[1,32,512]{2,1,0:T(8,128)(2,1)S(1)} %copy-done.3), kind=kOutput, calls=%fused_computation.3 | convolution fusion | flops 142884864 | bytes 5013504 | tf_op jit(solution)/shard_map/dot_general | solution.py:70
  145.6 1.9 convolution_convert_fusion.4
  148.5 2.1 reshape.98
  150.5 3.6 %all-to-all-start.1 = ((bf16[8,96,512]{2,1,0:T(8,128)(2,1)}), bf16[8,96,512]{2,1,0:T(8,128)(2,1)S(1)}, u32[]{:S(2)}, u32[]{:S(2)}) async-start(bf16[8,96,512]{2,1,0:T(8,128)(2,1)} %reshape.98), calls=%async_computation.2 | async-start | bytes 1572864 | tf_op jit(solution)/shard_map/all_to_all | solution.py:89
  154.1 5.7 %reduce-scatter.8.cloned.1.call-done = bf16[1,8,512]{2,1,0:T(8,128)(2,1)} async-done(((bf16[1,32,512]{2,1,0:T(8,128)(2,1)}), bf16[1,8,512]{2,1,0:T(8,128)(2,1)}) %reduce-scatter.8.cloned.1.call-update) | async-done | bytes 8208 | tf_op jit(solution)/shard_map/reduce_scatter | solution.py:96
  159.8 1.3 convert_element_type.68
  161.1 22.9 %reduce-scatter.6.cloned.1.call-done = bf16[1,32,2048]{2,1,0:T(8,128)(2,1)} async-done(((bf16[1,32,8192]{2,1,0:T(8,128)(2,1)}), bf16[1,32,2048]{2,1,0:T(8,128)(2,1)}) %reduce-scatter.6.cloned.1.call-update) | async-done | bytes 131088 | tf_op jit(solution)/shard_map/reduce_scatter | solution.py:93
  184.0 1.6 convert_element_type.65
  185.7 64.8 %reduce-scatter.4.cloned.1.call-done = bf16[96,512]{1,0:T(8,128)(2,1)} async-done(((bf16[768,512]{1,0:T(8,128)(2,1)}), bf16[96,512]{1,0:T(8,128)(2,1)}) %reduce-scatter.4.cloned.1.call-update) | async-done | bytes 98320 | tf_op jit(solution)/shard_map/reduce_scatter | solution.py:76
  250.5 1.6 add_convert_fusion
  (27 shorter events, 1.9 us)
Async XLA Ops:
  7.2 138.4 %copy-start = (bf16[1024,512]{1,0:T(8,128)(2,1)S(1)}, bf16[1024,512]{1,0:T(8,128)(2,1)}, u32[]{:S(2)}) copy-start(bf16[1024,512]{1,0:T(8,128)(2,1)} %param.8) | copy-start | bytes 3145732
  26.8 7.4 %copy-start.4 = (bf16[768,64]{0,1:T(8,128)(2,1)S(1)}, bf16[768,64]{0,1:T(8,128)(2,1)}, u32[]{:S(2)}) copy-start(bf16[768,64]{0,1:T(8,128)(2,1)} %param.7) | copy-start | bytes 294916
  26.8 104.4 %copy-start.2 = (bf16[1,32,8192]{2,1,0:T(8,128)(2,1)S(1)}, bf16[1,32,8192]{2,1,0:T(8,128)(2,1)}, u32[]{:S(2)}) copy-start(bf16[1,32,8192]{2,1,0:T(8,128)(2,1)} %param.9) | copy-start | bytes 1572868
  26.8 100.7 %all-to-all-start = ((bf16[8,256,1024]{1,2,0:T(8,128)(2,1)}), bf16[8,256,1024]{1,2,0:T(8,128)(2,1)}, u32[]{:S(2)}, u32[]{:S(2)}) async-start(bf16[8,256,1024]{1,2,0:T(8,128)(2,1)} %copy.15), calls=%async_computation.1 | async-start | bytes 8388608 | tf_op jit(solution)/shard_map/all_to_all | solution.py:51
  34.2 106.9 %copy-start.3 = (bf16[1,32,512]{2,1,0:T(8,128)(2,1)S(1)}, bf16[1,32,512]{2,1,0:T(8,128)(2,1)}, u32[]{:S(2)}) copy-start(bf16[1,32,512]{2,1,0:T(8,128)(2,1)} %param.10) | copy-start | bytes 98308
  127.5 12.7 %all-to-all-start.2 = ((bf16[8,256,64]{1,2,0:T(8,128)(2,1)}), bf16[8,256,64]{1,2,0:T(8,128)(2,1)S(1)}, u32[]{:S(2)}, u32[]{:S(2)}) async-start(bf16[8,256,64]{1,2,0:T(8,128)(2,1)} %copy.17), calls=%async_computation.3 | async-start | bytes 524288 | tf_op jit(solution)/shard_map/all_to_all | solution.py:52
  131.1 28.7 %reduce-scatter.8.cloned.1.call-start = ((), (), s32[]{:S(2)}) async-start(), calls=%async_computation.8 | async-start | bytes 40960 | tf_op jit(solution)/shard_map/reduce_scatter | solution.py:96
  131.2 14.4 %copy-start.1 = (bf16[768,1024]{1,0:T(8,128)(2,1)S(1)}, bf16[768,1024]{1,0:T(8,128)(2,1)}, u32[]{:S(2)}) copy-start(bf16[768,1024]{1,0:T(8,128)(2,1)} %param.6) | copy-start | bytes 4718596
  141.0 43.0 %reduce-scatter.6.cloned.1.call-start = ((), (), s32[]{:S(2)}) async-start(), calls=%async_computation.7 | async-start | bytes 655360 | tf_op jit(solution)/shard_map/reduce_scatter | solution.py:93
  145.5 105.0 %reduce-scatter.4.cloned.1.call-start = ((), (), s32[]{:S(2)}) async-start(), calls=%async_computation.6 | async-start | bytes 884736 | tf_op jit(solution)/shard_map/reduce_scatter | solution.py:76
  150.5 35.1 %all-to-all-start.1 = ((bf16[8,96,512]{2,1,0:T(8,128)(2,1)}), bf16[8,96,512]{2,1,0:T(8,128)(2,1)S(1)}, u32[]{:S(2)}, u32[]{:S(2)}) async-start(bf16[8,96,512]{2,1,0:T(8,128)(2,1)} %reshape.98), calls=%async_computation.2 | async-start | bytes 1572864 | tf_op jit(solution)/shard_map/all_to_all | solution.py:89
Sparse Core Ops, SparseCore 0:
  141.2 18.5 reduce-scatter.7
  162.3 21.6 reduce-scatter.5
  187.3 63.1 reduce-scatter.3
where the time goes:
time: 259 us
  waiting for transfers between devices  191 us (74%)
  local copies, waits for them, and re-layouts  18.8 us (7%)
  starting transfers between devices  14.8 us (6%)
  matrix products  14.4 us (6%)
  between operations  13.9 us (5%)
  other arithmetic  6.27 us (2%)
    all_to_all x1, waiting for transfers between devices, shards(): lax.all_to_all(send_tokens, 'tensor', split_axis=0, concat_axis=2, tiled=...  91.2 us
    reduce_scatter x1, waiting for transfers between devices, shards(): lax.psum_scatter(jnp.dot(tokens, frozen_value_weight, preferred_element_t...  64.8 us
    reduce_scatter x1, waiting for transfers between devices, shards(): lax.psum_scatter(local_down[None].astype(jnp.bfloat16), 'dp', scatter_dim...  22.9 us
    reshape x2, local copies, waits for them, and re-layouts, shards(): send_tokens = send_tokens.reshape(tensor_size, CAP * BLK, feature_width)  11.3 us
    all_to_all x1, starting transfers between devices, shards(): lax.all_to_all(send_tokens, 'tensor', split_axis=0, concat_axis=2, tiled=...  7.41 us
    all_to_all x1, waiting for transfers between devices, shards(): lax.all_to_all(send_cot, 'tensor', split_axis=0, concat_axis=2, tiled=True)  5.91 us
    reduce_scatter x1, waiting for transfers between devices, shards(): lax.psum_scatter(member_up_weight[None].astype(jnp.bfloat16), 'dp', scatt...  5.65 us
  transfers between devices with their start and end apart: 6, of which 5 were waited for; matrix products, arithmetic and copies ran while one was open for 7% of the time, Pallas kernels for 0%

commit v1 on v0

--- a/solution.py
+++ b/solution.py
@@ -8,6 +8,13 @@
 adapter_scale = 2.0
 contract_trailing = (((1,), (1,)), ((), ()))
 contract_leading = (((0,), (0,)), ((), ()))
+
+
+def swap_blocks(x, axis, split, join):
+    n_dev = lax.axis_size(axis)
+    tiles = jnp.stack(jnp.split(x, n_dev, axis=split), axis=0)
+    tiles = lax.all_to_all(tiles, axis, split_axis=0, concat_axis=0)
+    return jnp.concatenate(tiles, axis=join)
 
 
 def slot_table(member_ids, tensor_size):
@@ -48,7 +55,7 @@
     )
     send_cot = send_cot.reshape(tensor_size, CAP * BLK, cot_width)
     got_tokens, got_cot = (
-        lax.all_to_all(send_tokens, "tensor", split_axis=0, concat_axis=2, tiled=True),
+        swap_blocks(send_tokens, "tensor", 0, 2),
         lax.all_to_all(send_cot, "tensor", split_axis=0, concat_axis=2, tiled=True),
     )
     slot_tokens = got_tokens[0]

time: 259 us -> 289 us (1.12)
  local copies, waits for them, and re-layouts: 18.8 us -> 50.1 us
    another operation x0 -> x17, local copies, waits for them, and re-layouts: none -> 31.7 us  [swap_blocks(): tiles = jnp.stack(jnp.split(x, n_dev, axis=split), axis=0)]
    reshape x2 -> x0, local copies, waits for them, and re-layouts: 11.3 us -> none  [shards(): send_tokens = send_tokens.reshape(tensor_size, CAP * BLK, feature_width)]
    unnamed x11 -> x32, local copies, waits for them, and re-layouts: 0.19 us -> 7.14 us
    split x0 -> x1, local copies, waits for them, and re-layouts: none -> 3.9 us  [swap_blocks(): tiles = jnp.stack(jnp.split(x, n_dev, axis=split), axis=0)]
  transfers between devices with their start and end apart: 6 -> 6, of which waited for: 5 -> 5; matrix products, arithmetic and copies ran while one was open for 7% -> 6% of each run, Pallas kernels for 0% -> 0%
where the time goes in v1:
time: 289 us; the launch traced here: 288 us
  waiting for transfers between devices  190 us (66%)
  local copies, waits for them, and re-layouts  50.1 us (17%)
  starting transfers between devices  14.9 us (5%)
  between operations  13.9 us (5%)
  matrix products  12.4 us (4%)
  other arithmetic  6.27 us (2%)
    all_to_all x1, waiting for transfers between devices, swap_blocks(): tiles = lax.all_to_all(tiles, axis, split_axis=0, concat_axis=0)  91.2 us
    reduce_scatter x1, waiting for transfers between devices, shards(): lax.psum_scatter(jnp.dot(tokens, frozen_value_weight, preferred_element_t...  64.9 us
    another operation x17, local copies, waits for them, and re-layouts, swap_blocks(): tiles = jnp.stack(jnp.split(x, n_dev, axis=split), axis=0)  31.7 us
    reduce_scatter x1, waiting for transfers between devices, shards(): lax.psum_scatter(local_down[None].astype(jnp.bfloat16), 'dp', scatter_dim...  22.9 us
    all_to_all x1, starting transfers between devices, swap_blocks(): tiles = lax.all_to_all(tiles, axis, split_axis=0, concat_axis=0)  7.41 us
    unnamed x32, local copies, waits for them, and re-layouts  7.14 us
  transfers between devices with their start and end apart: 6, of which 5 were waited for; matrix products, arithmetic and copies ran while one was open for 6% of the time, Pallas kernels for 0%

profile of v1, /device:TPU:0, one launch (start us, length us, event | category | flops | bytes accessed | tf_op | source)
XLA Modules:
  0.0 288.0 jit_solution(7152542226470455341)
XLA Ops:
  8.9 3.4 %reshape.111 = bf16[6,131072]{1,0:T(8,128)(2,1)S(1)} reshape(bf16[768,1024]{1,0:T(8,128)(2,1)} %param.6) | data formatting | bytes 3145728 | tf_op jit(solution)/shard_map/reshape | solution.py:47
  13.5 3.9 %fusion.15 = (bf16[2,131072]{1,0:T(2,128)(2,1)S(1)}, bf16[2,131072]{1,0:T(2,128)(2,1)S(1)}, bf16[2,131072]{1,0:T(2,128)(2,1)S(1)}, bf16[2,131072]{1,0:T(2,128)(2...) fusion(bf16[16,131072]{1,0:T(8,128)(2,1)S(1)} %convolution_conv, ...), kind=kLoop, calls=%fused_computation.38 | loop fusion | bytes 8388608 | tf_op jit(solution)/shard_map/split | solution.py:15
  17.4 2.3 stack.27
  19.7 2.0 copy.30
  23.6 2.3 stack.28
  27.9 2.3 stack.29
  30.2 2.0 copy.32
  32.3 2.3 stack.30
  34.6 2.1 copy.33
  38.0 2.1 copy.34
  41.3 2.1 copy.35
  44.7 2.1 copy.36
  48.1 2.1 copy.37
  56.1 7.4 %all-to-all-start = ((bf16[8,1,256,1024]{2,3,1,0:T(8,128)(2,1)}), bf16[8,1,256,1024]{2,3,1,0:T(8,128)(2,1)}, u32[]{:S(2)}, u32[]{:S(2)}) async-start(bf16[8,1,256,1024]{2,3,1,0:T(8,128)(2,1)} %constant_dynamic-update-slice_fusion), calls=%async_computation.1 | async-start | bytes 8388608 | tf_op jit(solution)/shard_map/all_to_all | solution.py:16
  65.5 91.2 %all-to-all-done = bf16[8,1,256,1024]{2,3,1,0:T(8,128)(2,1)} async-done(((bf16[8,1,256,1024]{2,3,1,0:T(8,128)(2,1)}), bf16[8,1,256,1024]{2,3,1,0:T(8,128)(2,1)}, u32[]{:S(2)}, u32[]{:S(2)}) %all-to-all-start) | async-done | bytes 4194336 | tf_op jit(solution)/shard_map/all_to_all | solution.py:16
  156.8 3.6 %all-to-all-start.2 = ((bf16[8,256,64]{1,2,0:T(8,128)(2,1)}), bf16[8,256,64]{1,2,0:T(8,128)(2,1)S(1)}, u32[]{:S(2)}, u32[]{:S(2)}) async-start(bf16[8,256,64]{1,2,0:T(8,128)(2,1)} %copy.40), calls=%async_computation.3 | async-start | bytes 524288 | tf_op jit(solution)/shard_map/all_to_all | solution.py:59
  160.7 3.1 %convolution_convert_fusion.5 = bf16[256,32]{0,1:T(8,128)(2,1)S(1)} fusion(bf16[256,8192]{0,1:T(8,128)(2,1)} %bitcast.4, bf16[1,32,8192]{2,1,0:T(8,128)(2,1)S(1)} %copy-done.9), kind=kOutput, calls=%fused_computation.14 | convolution fusion | flops 134225920 | bytes 4734976 | tf_op jit(solution)/shard_map/dot_general | solution.py:65
  163.8 5.7 %all-to-all-done.2 = bf16[8,256,64]{1,2,0:T(8,128)(2,1)S(1)} async-done(((bf16[8,256,64]{1,2,0:T(8,128)(2,1)}), bf16[8,256,64]{1,2,0:T(8,128)(2,1)S(1)}, u32[]{:S(2)}, u32[]{:S(2)}) %all-to-all-start.2) | async-done | bytes 262176 | tf_op jit(solution)/shard_map/all_to_all | solution.py:59
  170.4 4.4 %fusion = bf16[1,32,8192]{2,1,0:T(8,128)(2,1)} fusion(bf16[256,8192]{0,1:T(8,128)(2,1)} %bitcast.4, bf16[256,512]{0,1:T(8,128)(2,1)S(1)} %bitcast.41, bf16[1,32,512]{2,1,0:T(8,128)(2,1)S(1)} %copy-done.10), kind=kOutput, calls=%fused_computation.3 | convolution fusion | flops 142884864 | bytes 5013504 | tf_op jit(solution)/shard_map/dot_general | solution.py:77
  177.8 2.1 reshape.114
  179.9 3.6 %all-to-all-start.1 = ((bf16[8,96,512]{2,1,0:T(8,128)(2,1)}), bf16[8,96,512]{2,1,0:T(8,128)(2,1)S(1)}, u32[]{:S(2)}, u32[]{:S(2)}) async-start(bf16[8,96,512]{2,1,0:T(8,128)(2,1)} %reshape.114), calls=%async_computation.2 | async-start | bytes 1572864 | tf_op jit(solution)/shard_map/all_to_all | solution.py:96
  183.5 5.6 %reduce-scatter.8.cloned.1.call-done = bf16[1,8,512]{2,1,0:T(8,128)(2,1)} async-done(((bf16[1,32,512]{2,1,0:T(8,128)(2,1)}), bf16[1,8,512]{2,1,0:T(8,128)(2,1)}) %reduce-scatter.8.cloned.1.call-update) | async-done | bytes 8208 | tf_op jit(solution)/shard_map/reduce_scatter | solution.py:103
  190.4 22.9 %reduce-scatter.6.cloned.1.call-done = bf16[1,32,2048]{2,1,0:T(8,128)(2,1)} async-done(((bf16[1,32,8192]{2,1,0:T(8,128)(2,1)}), bf16[1,32,2048]{2,1,0:T(8,128)(2,1)}) %reduce-scatter.6.cloned.1.call-update) | async-done | bytes 131088 | tf_op jit(solution)/shard_map/reduce_scatter | solution.py:100
  215.0 64.9 %reduce-scatter.4.cloned.1.call-done = bf16[96,512]{1,0:T(8,128)(2,1)} async-done(((bf16[768,512]{1,0:T(8,128)(2,1)}), bf16[96,512]{1,0:T(8,128)(2,1)}) %reduce-scatter.4.cloned.1.call-update) | async-done | bytes 98320 | tf_op jit(solution)/shard_map/reduce_scatter | solution.py:83
  (64 shorter events, 28.4 us)
Async XLA Ops:
  7.2 167.7 %copy-start = (bf16[1024,512]{1,0:T(8,128)(2,1)S(1)}, bf16[1024,512]{1,0:T(8,128)(2,1)}, u32[]{:S(2)}) copy-start(bf16[1024,512]{1,0:T(8,128)(2,1)} %param.8) | copy-start | bytes 3145732
  38.0 12.2 %copy-start.1 = (bf16[1,1,256,1024]{2,3,1,0:T(8,128)(2,1)S(1)}, bf16[1,1,256,1024]{2,3,1,0:T(8,128)(2,1)}, u32[]{:S(2)}) copy-start(bf16[1,1,256,1024]{2,3,1,0:T(8,128)(2,1)} %copy.31) | copy-start | bytes 1572868
  41.3 9.7 %copy-start.2 = (bf16[1,1,256,1024]{2,3,1,0:T(8,128)(2,1)S(1)}, bf16[1,1,256,1024]{2,3,1,0:T(8,128)(2,1)}, u32[]{:S(2)}) copy-start(bf16[1,1,256,1024]{2,3,1,0:T(8,128)(2,1)} %copy.32) | copy-start | bytes 1572868
  44.7 7.2 %copy-start.3 = (bf16[1,1,256,1024]{2,3,1,0:T(8,128)(2,1)S(1)}, bf16[1,1,256,1024]{2,3,1,0:T(8,128)(2,1)}, u32[]{:S(2)}) copy-start(bf16[1,1,256,1024]{2,3,1,0:T(8,128)(2,1)} %copy.33) | copy-start | bytes 1572868
  48.1 4.6 %copy-start.4 = (bf16[1,1,256,1024]{2,3,1,0:T(8,128)(2,1)S(1)}, bf16[1,1,256,1024]{2,3,1,0:T(8,128)(2,1)}, u32[]{:S(2)}) copy-start(bf16[1,1,256,1024]{2,3,1,0:T(8,128)(2,1)} %copy.34) | copy-start | bytes 1572868
  50.2 3.4 %copy-start.5 = (bf16[1,1,256,1024]{2,3,1,0:T(8,128)(2,1)S(1)}, bf16[1,1,256,1024]{2,3,1,0:T(8,128)(2,1)}, u32[]{:S(2)}) copy-start(bf16[1,1,256,1024]{2,3,1,0:T(8,128)(2,1)} %copy.35) | copy-start | bytes 1572868
  50.2 4.2 %copy-start.6 = (bf16[1,1,256,1024]{2,3,1,0:T(8,128)(2,1)S(1)}, bf16[1,1,256,1024]{2,3,1,0:T(8,128)(2,1)}, u32[]{:S(2)}) copy-start(bf16[1,1,256,1024]{2,3,1,0:T(8,128)(2,1)} %copy.36) | copy-start | bytes 1572868
  50.2 5.1 %copy-start.7 = (bf16[1,1,256,1024]{2,3,1,0:T(8,128)(2,1)S(1)}, bf16[1,1,256,1024]{2,3,1,0:T(8,128)(2,1)}, u32[]{:S(2)}) copy-start(bf16[1,1,256,1024]{2,3,1,0:T(8,128)(2,1)} %copy.37) | copy-start | bytes 1572868
  56.1 7.4 %copy-start.11 = (bf16[768,64]{0,1:T(8,128)(2,1)S(1)}, bf16[768,64]{0,1:T(8,128)(2,1)}, u32[]{:S(2)}) copy-start(bf16[768,64]{0,1:T(8,128)(2,1)} %param.7) | copy-start | bytes 294916
  56.1 104.6 %copy-start.9 = (bf16[1,32,8192]{2,1,0:T(8,128)(2,1)S(1)}, bf16[1,32,8192]{2,1,0:T(8,128)(2,1)}, u32[]{:S(2)}) copy-start(bf16[1,32,8192]{2,1,0:T(8,128)(2,1)} %param.9) | copy-start | bytes 1572868
  56.1 100.7 %all-to-all-start = ((bf16[8,1,256,1024]{2,3,1,0:T(8,128)(2,1)}), bf16[8,1,256,1024]{2,3,1,0:T(8,128)(2,1)}, u32[]{:S(2)}, u32[]{:S(2)}) async-start(bf16[8,1,256,1024]{2,3,1,0:T(8,128)(2,1)} %constant_dynamic-update-slice_fusion), calls=%async_computation.1 | async-start | bytes 8388608 | tf_op jit(solution)/shard_map/all_to_all | solution.py:16
  63.5 106.9 %copy-start.10 = (bf16[1,32,512]{2,1,0:T(8,128)(2,1)S(1)}, bf16[1,32,512]{2,1,0:T(8,128)(2,1)}, u32[]{:S(2)}) copy-start(bf16[1,32,512]{2,1,0:T(8,128)(2,1)} %param.10) | copy-start | bytes 98308
  156.8 12.7 %all-to-all-start.2 = ((bf16[8,256,64]{1,2,0:T(8,128)(2,1)}), bf16[8,256,64]{1,2,0:T(8,128)(2,1)S(1)}, u32[]{:S(2)}, u32[]{:S(2)}) async-start(bf16[8,256,64]{1,2,0:T(8,128)(2,1)} %copy.40), calls=%async_computation.3 | async-start | bytes 524288 | tf_op jit(solution)/shard_map/all_to_all | solution.py:59
  160.4 28.7 %reduce-scatter.8.cloned.1.call-start = ((), (), s32[]{:S(2)}) async-start(), calls=%async_computation.8 | async-start | bytes 40960 | tf_op jit(solution)/shard_map/reduce_scatter | solution.py:103
  160.7 14.2 %copy-start.8 = (bf16[768,1024]{1,0:T(8,128)(2,1)S(1)}, bf16[768,1024]{1,0:T(8,128)(2,1)}, u32[]{:S(2)}) copy-start(bf16[768,1024]{1,0:T(8,128)(2,1)} %param.6) | copy-start | bytes 4718596
  170.3 43.0 %reduce-scatter.6.cloned.1.call-start = ((), (), s32[]{:S(2)}) async-start(), calls=%async_computation.7 | async-start | bytes 655360 | tf_op jit(solution)/shard_map/reduce_scatter | solution.py:100
  174.8 105.1 %reduce-scatter.4.cloned.1.call-start = ((), (), s32[]{:S(2)}) async-start(), calls=%async_computation.6 | async-start | bytes 884736 | tf_op jit(solution)/shard_map/reduce_scatter | solution.py:83
  179.9 35.0 %all-to-all-start.1 = ((bf16[8,96,512]{2,1,0:T(8,128)(2,1)}), bf16[8,96,512]{2,1,0:T(8,128)(2,1)S(1)}, u32[]{:S(2)}, u32[]{:S(2)}) async-start(bf16[8,96,512]{2,1,0:T(8,128)(2,1)} %reshape.114), calls=%async_computation.2 | async-start | bytes 1572864 | tf_op jit(solution)/shard_map/all_to_all | solution.py:96
Sparse Core Ops, SparseCore 0:
  170.5 18.5 reduce-scatter.7
  191.6 21.6 reduce-scatter.5
  216.6 63.2 reduce-scatter.3
